TPU v7x, 512 devices: a whole 4x8x8 slice. The times are simulated.
512 devices in a mesh: row: 8 (over z_lo, core), col: 8 (over x, z_hi), tm: 8 (over y).
Axes of the slice: x: 4, y: 8, z: 8 (z_hi: 2, z_lo: 4; z = z_hi * 4 + z_lo), core: 2. Of those that a mesh axis runs over, the one named last changes fastest.
Arguments:
- green_occ: bfloat16 [16, 256, 30720], P('tm', 'row', 'col'), may hold values from -6 to 6
- green_virt: bfloat16 [16, 256, 30720], P('tm', 'row', 'col'), may hold values from -6 to 6
- adjoint_w: bfloat16 [16, 256, 30720], P(None, 'row', ('col', 'tm')), may hold values from -6 to 6
- grad_basis: float32 [3, 256], P(None, 'row'), may hold values from -6 to 6
- owner_map: int32 [30720], replicated, may hold values from 0 to 999
- block_offset: int32 [8], P('row'), may hold values from 0 to 30688
Outputs:
- chi_freq: bfloat16 [16, 256, 30720], P(None, 'row', ('col', 'tm'))
- forces: float32 [3, 1000], replicated
All inputs are finite; a program needn't handle non-finite values.
Results may differ from a plain program's by a relative error of at most 0.0085.
Values may be sent and summed in bfloat16 or wider, within the bound.
No kernel may reach another device: no remote copies, remote signals or barrier semaphores. Data moves between devices by JAX's collectives and lax.ppermute only.
A program may use at most 64 MiB of HBM per device.

v0:
```python
import math
import jax
import jax.numpy as jnp
from jax import lax
from jax.sharding import PartitionSpec as P

NG = 30720
NTAU = 16
NATOM = 1000


def cos_table(count):
    steps = jnp.arange(count).astype(jnp.float32)
    tau = 0.1 * jnp.power(jnp.float32(1.35), steps)
    omega = 0.15 * jnp.power(jnp.float32(1.35), steps)
    return jnp.cos(omega[:, None] * tau[None, :]) / 4.0


def on_device(green_occ, green_virt, adjoint_w, grad_basis, owner_map, block_offset):
    table = cos_table(NTAU)
    scale = 1.0 / math.sqrt(NTAU * NG)
    row_count = green_occ.shape[1]
    product = (green_occ.astype(jnp.float32) * green_virt.astype(jnp.float32)).astype(jnp.bfloat16)
    chi_freq = jnp.einsum(
        "kt,tnc->knc",
        table,
        lax.all_to_all(product, "tm", split_axis=2, concat_axis=0, tiled=True).astype(jnp.float32),
        precision=lax.Precision.HIGHEST,
    ).astype(jnp.bfloat16)
    partial_value = (
        jnp.sum(adjoint_w.astype(jnp.float32) * chi_freq.astype(jnp.float32), axis=(0, 2)) * scale
    )
    owners = lax.dynamic_slice_in_dim(owner_map, block_offset[0], row_count, 0)
    onehot = (owners[:, None] == jnp.arange(NATOM)[None, :]).astype(jnp.float32)
    energy = lax.psum(partial_value, ("col", "tm"))
    local_forces = jnp.dot(
        grad_basis * energy[None, :],
        onehot,
        precision=lax.Precision.HIGHEST,
        preferred_element_type=jnp.float32,
    )
    forces = lax.psum(local_forces, "row")
    return (chi_freq, forces)


def solution(mesh):
    in_specs = (
        P("tm", "row", "col"),
        P("tm", "row", "col"),
        P(None, "row", ("col", "tm")),
        P(None, "row"),
        P(),
        P("row"),
    )
    out_specs = (P(None, "row", ("col", "tm")), P())
    return jax.shard_map(
        on_device, mesh=mesh, in_specs=in_specs, out_specs=out_specs, check_vma=False
    )
```

profile of v0, /device:TPU:1, one launch (start us, length us, event | category | flops | bytes accessed | tf_op | source)
XLA Modules:
  0.0 282.4 jit_solution(8296169190990714850)
XLA Ops:
  0.6 1.3 multiply_convert_fusion
  1.9 1.4 copy.16
  3.3 2.5 reshape.19
  5.9 7.7 %all-to-all-start = ((bf16[8,2,15360]{2,1,0:T(2,128)(2,1)}), bf16[8,2,15360]{2,1,0:T(2,128)(2,1)S(1)}, u32[]{:S(2)}, u32[]{:S(2)}) async-start(bf16[8,2,15360]{2,1,0:T(2,128)(2,1)} %reshape.19), calls=%async_computation | async-start | bytes 983040 | tf_op jit(solution)/shard_map/all_to_all | solution.py:27
  14.2 0.8 dynamic_slice.3
  15.0 12.4 %all-to-all-done = bf16[8,2,15360]{2,1,0:T(2,128)(2,1)S(1)} async-done(((bf16[8,2,15360]{2,1,0:T(2,128)(2,1)}), bf16[8,2,15360]{2,1,0:T(2,128)(2,1)S(1)}, u32[]{:S(2)}, u32[]{:S(2)}) %all-to-all-start) | async-done | bytes 491552 | tf_op jit(solution)/shard_map/all_to_all | solution.py:27
  27.4 1.0 reshape.20
  28.4 0.0 copy-start
  28.4 1.5 copy.17
  29.9 0.0 copy-start.1
  29.9 0.4 all_to_all.16
  30.3 0.0 copy-done
  30.4 1.1 multiply_reduce_fusion
  31.5 1.1 copy.19
  32.5 196.4 %psum.14 = f32[32]{0:T(128)S(1)} all-reduce(f32[32]{0:T(128)S(1)} %broadcast_multiply_fusion), channel_id=1, replica_groups=mesh['row'=8,'col'=8,'tm'=8] {'col','tm'}, use_global_device_ids=true, to_apply=%region_1.0 | all-reduce | flops 32 | bytes 256 | tf_op jit(solution)/shard_map/psum | solution.py:35
  228.9 0.0 copy-done.1
  228.9 0.2 fusion
  229.1 53.3 %psum.15 = f32[3,1000]{1,0:T(4,128)} all-reduce(f32[3,1000]{1,0:T(4,128)S(1)} %fusion), channel_id=1, replica_groups=mesh['row'=8,'col'=8,'tm'=8] {'row'}, use_global_device_ids=true, to_apply=%region_2.0 | all-reduce | flops 3000 | bytes 24000 | tf_op jit(solution)/shard_map/psum | solution.py:42
  (2 shorter events, 0.0 us)
Async XLA Ops:
  5.9 21.5 %all-to-all-start = ((bf16[8,2,15360]{2,1,0:T(2,128)(2,1)}), bf16[8,2,15360]{2,1,0:T(2,128)(2,1)S(1)}, u32[]{:S(2)}, u32[]{:S(2)}) async-start(bf16[8,2,15360]{2,1,0:T(2,128)(2,1)} %reshape.19), calls=%async_computation | async-start | bytes 983040 | tf_op jit(solution)/shard_map/all_to_all | solution.py:27
  28.4 2.0 copy-start
  29.9 199.0 %copy-start.1 = (f32[3,32]{1,0:T(4,128)S(1)}, f32[3,32]{1,0:T(4,128)}, u32[]{:S(2)}) copy-start(f32[3,32]{1,0:T(4,128)} %param.9) | copy-start | bytes 1156
where the time goes:
time: 283 us; the launch traced here: 282 us
  blocking collectives  250 us (88%)
  waiting for transfers between devices  12.4 us (4%)
  local copies, waits for them, and re-layouts  8.71 us (3%)
  starting transfers between devices  7.65 us (3%)
    psum x1, blocking collectives, on_device(): energy = lax.psum(partial_value, ('col', 'tm'))  196 us
    psum x1, blocking collectives, on_device(): forces = lax.psum(local_forces, 'row')  53.3 us
    all_to_all x1, waiting for transfers between devices, on_device(): lax.all_to_all(product, 'tm', split_axis=2, concat_axis=0, tiled=True)  12.4 us
    all_to_all x1, starting transfers between devices, on_device(): lax.all_to_all(product, 'tm', split_axis=2, concat_axis=0, tiled=True)  7.65 us
  transfers between devices with their start and end apart: 1, of which 1 were waited for; matrix products, arithmetic and copies ran while one was open for 0% of the time, Pallas kernels for 0%

commit v1 on v0

--- a/solution.py
+++ b/solution.py
@@ -7,6 +7,11 @@
 NG = 30720
 NTAU = 16
 NATOM = 1000
+
+
+def axis_by_axis(array, one, other):
+    partial = lax.psum(array, one)
+    return lax.psum(partial, other)
 
 
 def cos_table(count):
@@ -32,7 +37,7 @@
     )
     owners = lax.dynamic_slice_in_dim(owner_map, block_offset[0], row_count, 0)
     onehot = (owners[:, None] == jnp.arange(NATOM)[None, :]).astype(jnp.float32)
-    energy = lax.psum(partial_value, ("col", "tm"))
+    energy = axis_by_axis(partial_value, "tm", "col")
     local_forces = jnp.dot(
         grad_basis * energy[None, :],
         onehot,

time: 283 us -> 112 us (0.40)
  the two profiles are of different devices: /device:TPU:1 before, /device:TPU:8 now
where the time goes in v1:
time: 112 us; the launch traced here: 111 us
  blocking collectives  77.1 us (69%)
  waiting for transfers between devices  12.2 us (11%)
  starting transfers between devices  9.21 us (8%)
  local copies, waits for them, and re-layouts  8.71 us (8%)
  between operations  1.36 us (1%)
  matrix products  1.31 us (1%)
  other arithmetic  1.3 us (1%)
    psum x1, blocking collectives, axis_by_axis(): return lax.psum(partial, other)  35 us
    psum x1, blocking collectives, on_device(): forces = lax.psum(local_forces, 'row')  26.5 us
    psum x1, blocking collectives, axis_by_axis(): partial = lax.psum(array, one)  15.6 us
    all_to_all x1, waiting for transfers between devices, on_device(): lax.all_to_all(product, 'tm', split_axis=2, concat_axis=0, tiled=True)  12.2 us
    all_to_all x1, starting transfers between devices, on_device(): lax.all_to_all(product, 'tm', split_axis=2, concat_axis=0, tiled=True)  9.21 us
    unnamed x7, local copies, waits for them, and re-layouts  4.61 us
  transfers between devices with their start and end apart: 1, of which 1 were waited for; matrix products, arithmetic and copies ran while one was open for 1% of the time, Pallas kernels for 0%

profile of v1, /device:TPU:8, one launch (start us, length us, event | category | flops | bytes accessed | tf_op | source)
XLA Modules:
  0.0 111.2 jit_solution(13592653235829732455)
XLA Ops:
  0.6 1.3 %multiply_convert_fusion = bf16[2,32,3840]{2,1,0:T(8,128)(2,1)S(1)} fusion(bf16[2,32,3840]{2,1,0:T(8,128)(2,1)} %param.7, bf16[2,32,3840]{2,1,0:T(8,128)(2,1)} %param.6), kind=kLoop, calls=%fused_computation.2 | loop fusion | flops 983040 | bytes 1474560 | tf_op jit(solution)/shard_map/convert_element_type | solution.py:28
  1.9 1.4 %copy.16 = bf16[2,32,3840]{1,0,2:T(2,128)(2,1)S(1)} copy(bf16[2,32,3840]{2,1,0:T(8,128)(2,1)S(1)} %multiply_convert_fusion) | data formatting | bytes 983040 | tf_op jit(solution)/shard_map/convert_element_type | solution.py:28
  3.3 2.5 %reshape.19 = bf16[8,2,15360]{2,1,0:T(2,128)(2,1)} reshape(bf16[3840,2,32]{2,1,0:T(2,128)(2,1)S(1)} %bitcast.16) | data formatting | bytes 983040
  5.9 9.2 %all-to-all-start = ((bf16[8,2,15360]{2,1,0:T(2,128)(2,1)}), bf16[8,2,15360]{2,1,0:T(2,128)(2,1)S(1)}, u32[]{:S(2)}, u32[]{:S(2)}) async-start(bf16[8,2,15360]{2,1,0:T(2,128)(2,1)} %reshape.19), calls=%async_computation | async-start | bytes 983040 | tf_op jit(solution)/shard_map/all_to_all | solution.py:32
  15.7 0.8 dynamic_slice.3
  16.5 12.2 %all-to-all-done = bf16[8,2,15360]{2,1,0:T(2,128)(2,1)S(1)} async-done(((bf16[8,2,15360]{2,1,0:T(2,128)(2,1)}), bf16[8,2,15360]{2,1,0:T(2,128)(2,1)S(1)}, u32[]{:S(2)}, u32[]{:S(2)}) %all-to-all-start) | async-done | bytes 491552 | tf_op jit(solution)/shard_map/all_to_all | solution.py:32
  28.8 1.0 reshape.20
  29.7 0.0 copy-start
  29.7 1.5 %copy.17 = bf16[2,32,8,480]{3,0,2,1:T(2,128)(2,1)S(1)} copy(bf16[2,32,8,480]{1,0,3,2:T(2,128)(2,1)S(1)} %bitcast.17) | data formatting | bytes 983040 | tf_op jit(solution)/shard_map/all_to_all | solution.py:32
  31.3 0.0 copy-start.1
  31.3 0.4 all_to_all.16
  31.7 0.0 copy-done
  31.7 1.1 multiply_reduce_fusion
  32.8 1.1 copy.19
  33.9 15.6 %psum.21 = f32[32]{0:T(128)S(1)} all-reduce(f32[32]{0:T(128)S(1)} %broadcast_multiply_fusion), channel_id=1, replica_groups=mesh['row'=8,'col'=8,'tm'=8] {'tm'}, use_global_device_ids=true, to_apply=%region_1.0 | all-reduce | flops 32 | bytes 256 | tf_op jit(solution)/shard_map/psum | solution.py:13
  49.5 35.0 %psum.22 = f32[32]{0:T(128)S(1)} all-reduce(f32[32]{0:T(128)S(1)} %psum.21), channel_id=1, replica_groups=mesh['row'=8,'col'=8,'tm'=8] {'col'}, use_global_device_ids=true, to_apply=%region_2.0 | all-reduce | flops 32 | bytes 256 | tf_op jit(solution)/shard_map/psum | solution.py:14
  84.5 0.0 copy-done.1
  84.5 0.2 fusion
  84.7 26.5 %psum.23 = f32[3,1000]{1,0:T(4,128)} all-reduce(f32[3,1000]{1,0:T(4,128)S(1)} %fusion), channel_id=1, replica_groups=mesh['row'=8,'col'=8,'tm'=8] {'row'}, use_global_device_ids=true, to_apply=%region_3.0 | all-reduce | flops 3000 | bytes 24000 | tf_op jit(solution)/shard_map/psum | solution.py:47
  (2 shorter events, 0.0 us)
Async XLA Ops:
  5.9 22.9 %all-to-all-start = ((bf16[8,2,15360]{2,1,0:T(2,128)(2,1)}), bf16[8,2,15360]{2,1,0:T(2,128)(2,1)S(1)}, u32[]{:S(2)}, u32[]{:S(2)}) async-start(bf16[8,2,15360]{2,1,0:T(2,128)(2,1)} %reshape.19), calls=%async_computation | async-start | bytes 983040 | tf_op jit(solution)/shard_map/all_to_all | solution.py:32
  29.7 2.0 %copy-start = (bf16[16,32,480]{2,1,0:T(8,128)(2,1)S(1)}, bf16[16,32,480]{2,1,0:T(8,128)(2,1)}, u32[]{:S(2)}) copy-start(bf16[16,32,480]{2,1,0:T(8,128)(2,1)} %param.8) | copy-start | bytes 1474564
  31.3 53.3 %copy-start.1 = (f32[3,32]{1,0:T(4,128)S(1)}, f32[3,32]{1,0:T(4,128)}, u32[]{:S(2)}) copy-start(f32[3,32]{1,0:T(4,128)} %param.9) | copy-start | bytes 1156
